TPU v7x, 128 devices: a whole 4x4x4 slice. The times are simulated.
128 devices in a mesh: loop: 16 (over y_lo, z, core), red: 8 (over y_hi, x).
Axes of the slice: x: 4, y: 4 (y_hi: 2, y_lo: 2; y = y_hi * 2 + y_lo), z: 4, core: 2. Of those that a mesh axis runs over, the one named last changes fastest.
Arguments:
- query_ids: int32 [512], replicated, may hold values from 0 to 8191
- layer_index: int32 [1], replicated, may hold values from 0 to 3
- gradient: bfloat16 [8192, 28672], P('loop', 'red'), may hold values from -6 to 6
- out_basis: bfloat16 [8192, 8192], P('loop'), may hold values from -0.0625 to 0.0625
- in_basis: bfloat16 [28672, 28672], P('red', 'loop'), may hold values from -0.03125 to 0.03125
- out_eigen: float32 [4, 8192], replicated, may hold values from 0.2 to 2
- in_eigen: float32 [4, 28672], P(None, 'loop'), may hold values from 0.2 to 2
Outputs:
- preconditioned: bfloat16 [512, 28672], P('loop', 'red')
All inputs are finite; a program needn't handle non-finite values.
Results may differ from a plain program's by a relative error of at most 0.0055.
Values may be sent and summed in bfloat16 or wider, within the bound.
No kernel may reach another device: no remote copies, remote signals or barrier semaphores. Data moves between devices by JAX's collectives and lax.ppermute only.
A program may use at most 128 MiB of HBM per device.

v0:
```python
import jax
import jax.numpy as jnp
from jax import lax
from jax.sharding import PartitionSpec as P

damping = 0.05


def per_device(query_ids, layer_index, gradient, out_basis, in_basis, out_eigen, in_eigen):
    selected = jnp.take(out_basis, query_ids, axis=1)
    local_rows = lax.dot_general(
        selected, gradient, (((0,), (0,)), ((), ())), preferred_element_type=jnp.float32
    )
    rows_w = lax.psum(local_rows, "loop").astype(jnp.bfloat16)
    eigen_rows = jnp.take(jnp.take(out_eigen, layer_index, axis=0)[0], query_ids)
    eigen_cols = jnp.take(in_eigen, layer_index, axis=0)[0]
    local_rot = jnp.dot(rows_w, in_basis, preferred_element_type=jnp.float32)
    rotated = lax.psum(local_rot, "red")
    scaled = (rotated / (eigen_rows[:, None] * eigen_cols[None, :] + damping)).astype(jnp.bfloat16)
    result = lax.psum_scatter(
        lax.dot_general(
            scaled, in_basis, (((1,), (1,)), ((), ())), preferred_element_type=jnp.float32
        ),
        "loop",
        scatter_dimension=0,
        tiled=True,
    )
    return result.astype(jnp.bfloat16)


def solution(mesh):
    return jax.shard_map(
        per_device,
        mesh=mesh,
        in_specs=(
            P(),
            P(),
            P("loop", "red"),
            P("loop", None),
            P("red", "loop"),
            P(),
            P(None, "loop"),
        ),
        out_specs=P("loop", "red"),
        check_vma=False,
    )
```

profile of v0, /device:TPU:4, one launch (start us, length us, event | category | flops | bytes accessed | tf_op | source)
XLA Modules:
  0.0 341.5 jit_solution(16668026155570244711)
XLA Ops:
  6.5 0.0 all-reduce.3.cloned.1.call-start
  7.2 0.7 compare_select_fusion
  7.9 0.9 broadcast_select_fusion
  8.8 3.1 gather_fusion.1
  12.0 0.7 broadcast_select_fusion.2
  12.7 11.9 %copy.9 = bf16[512,8192]{0,1:T(8,128)(2,1)} copy(bf16[512,8192]{1,0:T(8,128)(2,1)} %param.10) | data formatting | bytes 16777216 | tf_op args[3]
  24.6 6.4 %gather_fusion = bf16[512,512]{1,0:T(8,128)(2,1)S(1)} fusion(bf16[512,8192]{0,1:T(8,128)(2,1)} %copy.9, s32[1024]{0:T(1024)S(1)} %pad_clamp_fusion), kind=kCustom, calls=%fused_computation | custom fusion | bytes 1050624 | tf_op jit(solution)/shard_map/jit(_take)/gather | solution.py:10
  31.1 7.1 %fusion.6 = f32[512,3584]{1,0:T(8,128)} fusion(bf16[512,3584]{1,0:T(8,128)(2,1)} %param.9, bf16[512,512]{1,0:T(8,128)(2,1)S(1)} %gather_fusion, pred[512]{0:T(512)(128)(4,1)S(1)} %get-tuple-element.28), kind=kOutput, calls=%fused_computation.9 | convolution fusion | flops 1879310336 | bytes 11534848 | tf_op jit(solution)/shard_map/dot_general | solution.py:11
  38.2 93.1 %all-reduce.4 = bf16[512,3584]{1,0:T(8,128)(2,1)} all-reduce(f32[512,3584]{1,0:T(8,128)} %fusion.6), channel_id=1, replica_groups=mesh['loop'=16,'red'=8] {'loop'}, use_global_device_ids=true, to_apply=%region_0.1 | all-reduce | flops 1835008 | bytes 11010048 | tf_op jit(solution)/shard_map/psum | solution.py:14
  131.4 13.4 %fusion.13 = f32[512,1792]{1,0:T(8,128)} fusion(bf16[512,3584]{1,0:T(8,128)(2,1)} %all-reduce.4, bf16[3584,1792]{1,0:T(8,128)(2,1)} %param.11), kind=kOutput, calls=%fused_computation.22 | convolution fusion | flops 6576668672 | bytes 20185088 | tf_op jit(solution)/shard_map/dot_general | solution.py:17
  144.8 0.0 all-reduce.3.cloned.1.call-update
  144.8 0.0 reduce-scatter.2.cloned.1.call-start
  144.8 0.8 fusion.10
  145.6 99.3 %all-reduce.3.cloned.1.call-done = f32[512,1792]{1,0:T(8,128)} async-done(((f32[512,1792]{1,0:T(8,128)}), f32[512,1792]{1,0:T(8,128)}) %all-reduce.3.cloned.1.call-update) | async-done | bytes 3670032 | tf_op jit(solution)/shard_map/psum | solution.py:18
  244.9 12.9 %fusion.2 = f32[512,3584]{1,0:T(8,128)} fusion(bf16[3584,1792]{1,0:T(8,128)(2,1)} %param.11, f32[512,1792]{1,0:T(8,128)} %all-reduce.3.cloned.1.call-done, f32[1792]{0:T(1024)S(1)} %fusion.10, f32[512]{0:T(512)S(1)} %get-tuple-element.27), kind=kOutput, calls=%fused_computation.5 | convolution fusion | flops 6580338688 | bytes 23864320 | tf_op jit(solution)/shard_map/dot_general | solution.py:21
  257.8 0.0 reduce-scatter.2.cloned.1.call-update
  257.9 75.1 %reduce-scatter.2.cloned.1.call-done = f32[32,3584]{1,0:T(8,128)} async-done(((f32[512,3584]{1,0:T(8,128)}), f32[32,3584]{1,0:T(8,128)}) %reduce-scatter.2.cloned.1.call-update) | async-done | bytes 458768 | tf_op jit(solution)/shard_map/reduce_scatter | solution.py:20
  332.9 1.7 convert_element_type.11
  (1 shorter events, 0.0 us)
Async XLA Ops:
  6.5 238.4 %all-reduce.3.cloned.1.call-start = ((), (), s32[]{:S(2)}) async-start(), calls=%async_computation.1 | async-start | bytes 7340032 | tf_op jit(solution)/shard_map/psum | solution.py:18
  144.8 188.2 %reduce-scatter.2.cloned.1.call-start = ((), (), s32[]{:S(2)}) async-start(), calls=%async_computation.2 | async-start | bytes 7798784 | tf_op jit(solution)/shard_map/reduce_scatter | solution.py:20
Sparse Core Ops, SparseCore 0:
  144.9 99.9 all-reduce.2
  258.0 74.9 reduce-scatter.1
where the time goes:
time: 342 us
  waiting for transfers between devices  174 us (51%)
  blocking collectives  93.1 us (27%)
  matrix products  33.5 us (10%)
  local copies, waits for them, and re-layouts  21.5 us (6%)
  between operations  14.1 us (4%)
  other arithmetic  4.84 us (1%)
    psum x1, waiting for transfers between devices, per_device(): rotated = lax.psum(local_rot, 'red')  99.3 us
    psum x1, blocking collectives, per_device(): rows_w = lax.psum(local_rows, 'loop').astype(jnp.bfloat16)  93.1 us
    reduce_scatter x1, waiting for transfers between devices, per_device(): lax.psum_scatter(lax.dot_general(scaled, in_basis, (((1,), (1,)), ((), ()...  75.1 us
    dot_general x1, matrix products, per_device(): local_rot = jnp.dot(rows_w, in_basis, preferred_element_type=jnp.float32)  13.4 us
    dot_general x1, matrix products, per_device(): lax.dot_general(scaled, in_basis, (((1,), (1,)), ((), ())), preferred_ele...  12.9 us
    unnamed x1, local copies, waits for them, and re-layouts  11.9 us
    dot_general x1, matrix products, per_device(): lax.dot_general(selected, gradient, (((0,), (0,)), ((), ())), preferred_e...  7.14 us
  transfers between devices with their start and end apart: 2, of which 2 were waited for; matrix products, arithmetic and copies ran while one was open for 0% of the time, Pallas kernels for 0%

commit v1 on v0

--- a/solution.py
+++ b/solution.py
@@ -15,7 +15,7 @@
     eigen_rows = jnp.take(jnp.take(out_eigen, layer_index, axis=0)[0], query_ids)
     eigen_cols = jnp.take(in_eigen, layer_index, axis=0)[0]
     local_rot = jnp.dot(rows_w, in_basis, preferred_element_type=jnp.float32)
-    rotated = lax.psum(local_rot, "red")
+    rotated = jnp.sum(lax.all_gather(local_rot, "red"), axis=0)
     scaled = (rotated / (eigen_rows[:, None] * eigen_cols[None, :] + damping)).astype(jnp.bfloat16)
     result = lax.psum_scatter(
         lax.dot_general(

time: 342 us -> 552 us (1.61)
  waiting for transfers between devices: 174 us -> 371 us
  other arithmetic: 4.84 us -> 17.6 us
    all_gather x0 -> x1, waiting for transfers between devices: none -> 298 us  [per_device(): rotated = jnp.sum(lax.all_gather(local_rot, 'red'), axis=0)]
    psum x1 -> x0, waiting for transfers between devices: 99.3 us -> none  [per_device(): rotated = lax.psum(local_rot, 'red')]
    reduce_sum x0 -> x1, other arithmetic: none -> 12.8 us  [per_device(): rotated = jnp.sum(lax.all_gather(local_rot, 'red'), axis=0)]
where the time goes in v1:
time: 552 us; the launch traced here: 551 us
  waiting for transfers between devices  371 us (67%)
  blocking collectives  93.1 us (17%)
  matrix products  33.5 us (6%)
  local copies, waits for them, and re-layouts  21.5 us (4%)
  other arithmetic  17.6 us (3%)
  between operations  14.1 us (3%)
    all_gather x1, waiting for transfers between devices, per_device(): rotated = jnp.sum(lax.all_gather(local_rot, 'red'), axis=0)  298 us
    psum x1, blocking collectives, per_device(): rows_w = lax.psum(local_rows, 'loop').astype(jnp.bfloat16)  93.1 us
    reduce_scatter x1, waiting for transfers between devices, per_device(): lax.psum_scatter(lax.dot_general(scaled, in_basis, (((1,), (1,)), ((), ()...  72.5 us
    dot_general x1, matrix products, per_device(): local_rot = jnp.dot(rows_w, in_basis, preferred_element_type=jnp.float32)  13.4 us
    dot_general x1, matrix products, per_device(): lax.dot_general(scaled, in_basis, (((1,), (1,)), ((), ())), preferred_ele...  12.9 us
    reduce_sum x1, other arithmetic, per_device(): rotated = jnp.sum(lax.all_gather(local_rot, 'red'), axis=0)  12.8 us
    unnamed x1, local copies, waits for them, and re-layouts  11.9 us
  transfers between devices with their start and end apart: 2, of which 2 were waited for; matrix products, arithmetic and copies ran while one was open for 0% of the time, Pallas kernels for 0%

profile of v1, /device:TPU:4, one launch (start us, length us, event | category | flops | bytes accessed | tf_op | source)
XLA Modules:
  0.0 550.7 jit_solution(10373813082227248028)
XLA Ops:
  6.5 0.0 all-gather.3.cloned.1.call-start
  7.2 0.7 compare_select_fusion
  7.9 0.9 broadcast_select_fusion
  8.8 3.1 gather_fusion.1
  12.0 0.7 broadcast_select_fusion.2
  12.7 11.9 %copy.9 = bf16[512,8192]{0,1:T(8,128)(2,1)} copy(bf16[512,8192]{1,0:T(8,128)(2,1)} %param.10) | data formatting | bytes 16777216 | tf_op args[3]
  24.6 6.4 %gather_fusion = bf16[512,512]{1,0:T(8,128)(2,1)S(1)} fusion(bf16[512,8192]{0,1:T(8,128)(2,1)} %copy.9, s32[1024]{0:T(1024)S(1)} %pad_clamp_fusion), kind=kCustom, calls=%fused_computation | custom fusion | bytes 1050624 | tf_op jit(solution)/shard_map/jit(_take)/gather | solution.py:10
  31.1 7.1 %fusion.6 = f32[512,3584]{1,0:T(8,128)} fusion(bf16[512,3584]{1,0:T(8,128)(2,1)} %param.9, bf16[512,512]{1,0:T(8,128)(2,1)S(1)} %gather_fusion, pred[512]{0:T(512)(128)(4,1)S(1)} %get-tuple-element.28), kind=kOutput, calls=%fused_computation.9 | convolution fusion | flops 1879310336 | bytes 11534848 | tf_op jit(solution)/shard_map/dot_general | solution.py:11
  38.2 93.1 %all-reduce.1 = bf16[512,3584]{1,0:T(8,128)(2,1)} all-reduce(f32[512,3584]{1,0:T(8,128)} %fusion.6), channel_id=1, replica_groups=mesh['loop'=16,'red'=8] {'loop'}, use_global_device_ids=true, to_apply=%region_0.1 | all-reduce | flops 1835008 | bytes 11010048 | tf_op jit(solution)/shard_map/psum | solution.py:14
  131.4 13.4 %fusion.13 = f32[512,1792]{1,0:T(8,128)} fusion(bf16[512,3584]{1,0:T(8,128)(2,1)} %all-reduce.1, bf16[3584,1792]{1,0:T(8,128)(2,1)} %param.11), kind=kOutput, calls=%fused_computation.22 | convolution fusion | flops 6576668672 | bytes 20185088 | tf_op jit(solution)/shard_map/dot_general | solution.py:17
  144.8 0.0 all-gather.3.cloned.1.call-update
  144.8 0.0 reduce-scatter.2.cloned.1.call-start
  144.9 0.8 fusion.10
  145.7 298.2 %all-gather.3.cloned.1.call-done = f32[4096,1792]{1,0:T(8,128)} async-done(((f32[512,1792]{1,0:T(8,128)}), f32[4096,1792]{1,0:T(8,128)}) %all-gather.3.cloned.1.call-update) | async-done | bytes 29360144 | tf_op jit(solution)/shard_map/all_gather | solution.py:18
  443.9 12.8 %reduce_sum.9 = f32[512,1792]{1,0:T(8,128)} reduce(f32[8,512,1792]{2,1,0:T(8,128)} %bitcast.9, f32[]{:T(128)} %constant.54.clone.1), dimensions={0}, to_apply=%region_1.2 | reduce | flops 6422528 | bytes 33030148 | tf_op jit(solution)/shard_map/reduce_sum | solution.py:18
  456.6 12.9 %fusion.2 = f32[512,3584]{1,0:T(8,128)} fusion(bf16[3584,1792]{1,0:T(8,128)(2,1)} %param.11, f32[512,1792]{1,0:T(8,128)} %reduce_sum.9, f32[1792]{0:T(1024)S(1)} %fusion.10, f32[512]{0:T(512)S(1)} %get-tuple-element.27), kind=kOutput, calls=%fused_computation.5 | convolution fusion | flops 6580338688 | bytes 23864320 | tf_op jit(solution)/shard_map/dot_general | solution.py:21
  469.6 0.0 reduce-scatter.2.cloned.1.call-update
  469.6 72.5 %reduce-scatter.2.cloned.1.call-done = f32[32,3584]{1,0:T(8,128)} async-done(((f32[512,3584]{1,0:T(8,128)}), f32[32,3584]{1,0:T(8,128)}) %reduce-scatter.2.cloned.1.call-update) | async-done | bytes 458768 | tf_op jit(solution)/shard_map/reduce_scatter | solution.py:20
  542.1 1.7 convert_element_type.11
  (1 shorter events, 0.0 us)
Async XLA Ops:
  6.5 437.3 %all-gather.3.cloned.1.call-start = ((), (), s32[]{:S(2)}) async-start(), calls=%async_computation.2 | async-start | bytes 33030144 | tf_op jit(solution)/shard_map/all_gather | solution.py:18
  144.8 397.3 %reduce-scatter.2.cloned.1.call-start = ((), (), s32[]{:S(2)}) async-start(), calls=%async_computation.1 | async-start | bytes 7798784 | tf_op jit(solution)/shard_map/reduce_scatter | solution.py:20
Sparse Core Ops, SparseCore 0:
  144.9 298.8 all-gather.2
  469.7 72.3 reduce-scatter.1
